TPU v7x, 256 devices: a whole 4x4x8 slice. The times are simulated.
256 devices in a mesh: dp: 32 (over z_hi, y, core), tensor: 8 (over x, z_lo).
Axes of the slice: x: 4, y: 4, z: 8 (z_hi: 4, z_lo: 2; z = z_hi * 2 + z_lo), core: 2. Of those that a mesh axis runs over, the one named last changes fastest.
Arguments:
- hidden: bfloat16 [32, 1024, 28672], P('dp', None, 'tensor'), may hold values from -6 to 6
- grad_out: bfloat16 [32, 1024, 8192], P('dp', None, 'tensor'), may hold values from -30 to 30
- proj_in: bfloat16 [64, 28672], P(None, 'tensor'), may hold values from -0.03125 to 0.03125
- proj_out: bfloat16 [64, 8192], P(None, 'tensor'), may hold values from -0.0625 to 0.0625
Outputs:
- covariance: float32 [4096, 4096], P('dp', 'tensor')
All inputs are finite; a program needn't handle non-finite values.
Results may differ from a plain program's by a relative error of at most 0.0003.
Values sent between devices are 32-bit elements; how exact they have to be, the bound alone decides.
No kernel may reach another device: no remote copies, remote signals or barrier semaphores. Data moves between devices by JAX's collectives and lax.ppermute only.
A program may use at most 64 MiB of HBM per device.

v0:
```python
import math
import jax
import jax.numpy as jnp
from jax import lax
from jax.sharding import PartitionSpec as P


def outer_sum(panels, width):
    left_side = panels[:, :, :width]
    right_side = panels[:, :, width:]
    return jnp.einsum(
        "sta,stb->sab",
        left_side,
        right_side,
        precision=lax.Precision.HIGHEST,
        preferred_element_type=jnp.float32,
    )


def shards(hidden, grad_out, proj_in, proj_out):
    seqs_here = hidden.shape[0]
    length = hidden.shape[1]
    width = proj_in.shape[0]
    inv_root = 1.0 / math.sqrt(length)
    in_panel = jnp.einsum("stf,af->sta", hidden, proj_in, preferred_element_type=jnp.float32)
    out_panel = jnp.einsum("ste,be->stb", grad_out, proj_out, preferred_element_type=jnp.float32)
    panels = jnp.concatenate([in_panel, out_panel], axis=2)
    summed = lax.psum(panels, "tensor")
    seq_outer = outer_sum(summed, width)
    flat_grads = (seq_outer * inv_root).reshape(seqs_here, width * width)
    total_len = width * width
    col_count = total_len // lax.axis_size("tensor")
    row_count = total_len // lax.axis_size("dp")
    col_begin = lax.axis_index("tensor") * col_count
    row_begin = lax.axis_index("dp") * row_count
    all_seqs = seqs_here * lax.axis_size("dp")
    gathered = lax.all_gather(flat_grads, "dp", axis=0, tiled=True)
    row_part = lax.dynamic_slice_in_dim(gathered, row_begin, row_count, 1)
    col_block = lax.dynamic_slice_in_dim(gathered, col_begin, col_count, 1)
    raw_block = jnp.dot(
        row_part.T, col_block, precision=lax.Precision.HIGHEST, preferred_element_type=jnp.float32
    )
    trace_total = jnp.sum(gathered * gathered)
    damping = 0.5 * trace_total / (all_seqs * total_len)
    row_ids = row_begin + lax.broadcasted_iota(jnp.int32, (row_count, col_count), 0)
    col_ids = col_begin + lax.broadcasted_iota(jnp.int32, (row_count, col_count), 1)
    diagonal = jnp.where(row_ids == col_ids, damping, jnp.float32(0.0))
    return raw_block / all_seqs + diagonal


def solution(mesh):
    placed = (
        P("dp", None, "tensor"),
        P("dp", None, "tensor"),
        P(None, "tensor"),
        P(None, "tensor"),
    )
    return jax.shard_map(
        shards, mesh=mesh, in_specs=placed, out_specs=P("dp", "tensor"), check_vma=False
    )
```

profile of v0, /device:TPU:1, one launch (start us, length us, event | category | flops | bytes accessed | tf_op | source)
XLA Modules:
  0.0 158.4 jit_solution(9999071487780403758)
XLA Ops:
  6.5 0.0 copy-start
  6.5 0.0 all-reduce.2.cloned.1.call-start
  6.5 1.6 %copy-done = bf16[1,1024,1024]{2,1,0:T(8,128)(2,1)S(1)} copy-done((bf16[1,1024,1024]{2,1,0:T(8,128)(2,1)S(1)}, bf16[1,1024,1024]{2,1,0:T(8,128)(2,1)}, u32[]{:S(2)}) %copy-start) | copy-done | bytes 2097176
  8.1 1.7 %fusion.4 = f32[1,1024,64]{1,2,0:T(8,128)S(1)} fusion(bf16[64,1024]{1,0:T(8,128)(2,1)} %param.7, bf16[1,1024,1024]{2,1,0:T(8,128)(2,1)S(1)} %copy-done), kind=kOutput, calls=%fused_computation.4 | convolution fusion | flops 134217728 | bytes 2490368 | tf_op jit(solution)/shard_map/ste,be->stb/dot_general | solution.py:26
  9.8 5.4 %fusion.8 = f32[1,1024,64]{1,2,0:T(8,128)S(1)} fusion(bf16[64,3584]{1,0:T(8,128)(2,1)} %param.6, bf16[1,1024,3584]{2,1,0:T(8,128)(2,1)} %param.4), kind=kOutput, calls=%fused_computation.7 | convolution fusion | flops 469762048 | bytes 8060928 | tf_op jit(solution)/shard_map/stf,af->sta/dot_general | solution.py:25
  15.2 0.9 pad_maximum_fusion
  16.1 0.0 all-reduce.2.cloned.1.call-update
  16.1 79.5 %all-reduce.2.cloned.1.call-done = f32[1,1024,128]{1,2,0:T(8,128)} async-done(((f32[1,1024,128]{1,2,0:T(8,128)}), f32[1,1024,128]{1,2,0:T(8,128)}) %all-reduce.2.cloned.1.call-update) | async-done | bytes 524304 | tf_op jit(solution)/shard_map/psum | solution.py:28
  95.6 1.4 convolution_multiply_fusion.1
  97.0 0.1 reshape.25
  97.1 51.0 %all-gather = f32[32,1,4096]{2,1,0:T(1,128)S(1)} all-gather(f32[1,1,4096]{2,1,0:T(1,128)S(1)} %reshape.25), channel_id=1, replica_groups=mesh['dp'=32,'tensor'=8] {'dp'}, dimensions={0}, use_global_device_ids=true | all-gather | bytes 540672 | tf_op jit(solution)/shard_map/all_gather | solution.py:37
  148.1 1.7 %multiply_reduce_fusion = f32[]{:T(128)} fusion(f32[32,1,4096]{2,1,0:T(1,128)S(1)} %all-gather), kind=kLoop, calls=%fused_computation.10 | loop fusion | flops 262143 | bytes 524292 | tf_op jit(solution)/shard_map/reduce_sum | solution.py:43
  150.5 1.1 fusion.7
  (4 shorter events, 0.1 us)
Async XLA Ops:
  6.5 1.6 %copy-start = (bf16[1,1024,1024]{2,1,0:T(8,128)(2,1)S(1)}, bf16[1,1024,1024]{2,1,0:T(8,128)(2,1)}, u32[]{:S(2)}) copy-start(bf16[1,1024,1024]{2,1,0:T(8,128)(2,1)} %param.5) | copy-start | bytes 6291460
  6.5 89.1 %all-reduce.2.cloned.1.call-start = ((), (), s32[]{:S(2)}) async-start(), calls=%async_computation | async-start | bytes 1048576 | tf_op jit(solution)/shard_map/psum | solution.py:28
Sparse Core Ops, SparseCore 0:
  16.2 79.3 all-reduce.1
where the time goes:
time: 159 us; the launch traced here: 158 us
  waiting for transfers between devices  79.5 us (50%)
  blocking collectives  51 us (32%)
  between operations  14.1 us (9%)
  matrix products  9.61 us (6%)
  other arithmetic  2.55 us (2%)
  local copies, waits for them, and re-layouts  1.72 us (1%)
    psum x1, waiting for transfers between devices, shards(): summed = lax.psum(panels, 'tensor')  79.5 us
    all_gather x1, blocking collectives, shards(): gathered = lax.all_gather(flat_grads, 'dp', axis=0, tiled=True)  51 us
    dot_general x1, matrix products, shards(): jnp.einsum('stf,af->sta', hidden, proj_in, preferred_element_type=jnp.flo...  5.43 us
  transfers between devices with their start and end apart: 1, of which 1 were waited for; matrix products, arithmetic and copies ran while one was open for 0% of the time, Pallas kernels for 0%

commit v1 on v0

--- a/solution.py
+++ b/solution.py
@@ -25,7 +25,8 @@
     in_panel = jnp.einsum("stf,af->sta", hidden, proj_in, preferred_element_type=jnp.float32)
     out_panel = jnp.einsum("ste,be->stb", grad_out, proj_out, preferred_element_type=jnp.float32)
     panels = jnp.concatenate([in_panel, out_panel], axis=2)
-    summed = lax.psum(panels, "tensor")
+    _deliver_sides = lambda load, axis_name: lax.all_gather(load, axis_name).sum(axis=0)
+    summed = _deliver_sides(panels, "tensor")
     seq_outer = outer_sum(summed, width)
     flat_grads = (seq_outer * inv_root).reshape(seqs_here, width * width)
     total_len = width * width

time: 159 us -> 174 us (1.094)
  waiting for transfers between devices: 79.5 us -> 97 us
  blocking collectives: 51 us -> 46.6 us
    all_gather x0 -> x1, waiting for transfers between devices: none -> 97 us  [shards(): lax.all_gather(load, axis_name).sum(axis=0)]
    psum x1 -> x0, waiting for transfers between devices: 79.5 us -> none  [shards(): summed = lax.psum(panels, 'tensor')]
    all_gather x1, blocking collectives: 51 us -> 46.6 us  [shards(): gathered = lax.all_gather(flat_grads, 'dp', axis=0, tiled=True)]
    reduce_sum x0 -> x1, other arithmetic: none -> 2.45 us  [shards(): lax.all_gather(load, axis_name).sum(axis=0)]
where the time goes in v1:
time: 174 us; the launch traced here: 173 us
  waiting for transfers between devices  97 us (56%)
  blocking collectives  46.6 us (27%)
  between operations  14.1 us (8%)
  matrix products  8.58 us (5%)
  other arithmetic  4.18 us (2%)
  local copies, waits for them, and re-layouts  2.91 us (2%)
    all_gather x1, waiting for transfers between devices, shards(): lax.all_gather(load, axis_name).sum(axis=0)  97 us
    all_gather x1, blocking collectives, shards(): gathered = lax.all_gather(flat_grads, 'dp', axis=0, tiled=True)  46.6 us
    dot_general x1, matrix products, shards(): jnp.einsum('stf,af->sta', hidden, proj_in, preferred_element_type=jnp.flo...  5.43 us
  transfers between devices with their start and end apart: 1, of which 1 were waited for; matrix products, arithmetic and copies ran while one was open for 0% of the time, Pallas kernels for 0%

profile of v1, /device:TPU:1, one launch (start us, length us, event | category | flops | bytes accessed | tf_op | source)
XLA Modules:
  0.0 173.4 jit_solution(16798493711488814419)
XLA Ops:
  6.5 0.0 copy-start
  6.5 0.0 all-gather.4.cloned.1.call-start
  6.5 1.6 copy-done
  8.1 1.7 fusion.4
  9.8 5.4 %fusion.8 = f32[1,1024,64]{1,2,0:T(8,128)S(1)} fusion(bf16[64,3584]{1,0:T(8,128)(2,1)} %param.6, bf16[1,1024,3584]{2,1,0:T(8,128)(2,1)} %param.4), kind=kOutput, calls=%fused_computation.7 | convolution fusion | flops 469762048 | bytes 8060928 | tf_op jit(solution)/shard_map/stf,af->sta/dot_general | solution.py:25
  15.3 1.0 copy.5
  16.3 0.0 all-gather.4.cloned.1.call-update
  16.3 97.0 %all-gather.4.cloned.1.call-done = f32[8,1024,128]{2,1,0:T(8,128)} async-done(((f32[1,1024,128]{2,1,0:T(8,128)}), f32[8,1024,128]{2,1,0:T(8,128)}) %all-gather.4.cloned.1.call-update) | async-done | bytes 4194320 | tf_op jit(solution)/shard_map/all_gather | solution.py:28
  113.3 2.4 %reduce.1 = f32[1024,128]{1,0:T(8,128)S(1)} reduce(f32[8,1024,128]{2,1,0:T(8,128)} %all-gather.4.cloned.1.call-done, f32[]{:T(128)} %constant.10.clone.1), dimensions={0}, to_apply=%region_0.0 | reduce | flops 917504 | bytes 4718596 | tf_op jit(solution)/shard_map/reduce_sum | solution.py:28
  115.8 0.2 copy.8
  116.0 0.4 convolution_multiply_fusion.1
  116.3 0.1 reshape.28
  116.4 46.6 %all-gather.1 = f32[32,1,4096]{2,1,0:T(1,128)S(1)} all-gather(f32[1,1,4096]{2,1,0:T(1,128)S(1)} %reshape.28), channel_id=1, replica_groups=mesh['dp'=32,'tensor'=8] {'dp'}, dimensions={0}, use_global_device_ids=true | all-gather | bytes 540672 | tf_op jit(solution)/shard_map/all_gather | solution.py:38
  163.0 1.7 multiply_reduce_fusion
  165.4 1.1 fusion.7
  (5 shorter events, 0.1 us)
Async XLA Ops:
  6.5 1.6 copy-start
  6.5 106.8 %all-gather.4.cloned.1.call-start = ((), (), s32[]{:S(2)}) async-start(), calls=%async_computation | async-start | bytes 4718592 | tf_op jit(solution)/shard_map/all_gather | solution.py:28
Sparse Core Ops, SparseCore 0:
  16.4 96.8 all-gather.3

commit v2 on v0

--- a/solution.py
+++ b/solution.py
@@ -3,6 +3,13 @@
 import jax.numpy as jnp
 from jax import lax
 from jax.sharding import PartitionSpec as P
+
+
+def exchange_gather(x, axis, dim):
+    size = lax.axis_size(axis)
+    tiles = jnp.stack([x for _ in range(size)])
+    tiles = lax.all_to_all(tiles, axis, split_axis=0, concat_axis=0)
+    return jnp.concatenate(tiles, axis=dim)
 
 
 def outer_sum(panels, width):
@@ -34,7 +41,7 @@
     col_begin = lax.axis_index("tensor") * col_count
     row_begin = lax.axis_index("dp") * row_count
     all_seqs = seqs_here * lax.axis_size("dp")
-    gathered = lax.all_gather(flat_grads, "dp", axis=0, tiled=True)
+    gathered = exchange_gather(flat_grads, "dp", 0)
     row_part = lax.dynamic_slice_in_dim(gathered, row_begin, row_count, 1)
     col_block = lax.dynamic_slice_in_dim(gathered, col_begin, col_count, 1)
     raw_block = jnp.dot(

time: 159 us -> 140 us (0.88)
  blocking collectives: 51 us -> 0 us
  waiting for transfers between devices: 79.5 us -> 97.3 us
  starting transfers between devices: 0.01 us -> 14.1 us
    all_gather x1 -> x0, blocking collectives: 51 us -> none  [shards(): gathered = lax.all_gather(flat_grads, 'dp', axis=0, tiled=True)]
    all_to_all x0 -> x1, waiting for transfers between devices: none -> 17.8 us  [exchange_gather(): tiles = lax.all_to_all(tiles, axis, split_axis=0, concat_axis=0)]
    all_to_all x0 -> x1, starting transfers between devices: none -> 14.1 us  [exchange_gather(): tiles = lax.all_to_all(tiles, axis, split_axis=0, concat_axis=0)]
  transfers between devices with their start and end apart: 1 -> 2, of which waited for: 1 -> 2; matrix products, arithmetic and copies ran while one was open for 0% -> 0% of each run, Pallas kernels for 0% -> 0%
where the time goes in v2:
time: 140 us
  waiting for transfers between devices  97.3 us (70%)
  starting transfers between devices  14.1 us (10%)
  between operations  14.1 us (10%)
  matrix products  9.61 us (7%)
  local copies, waits for them, and re-layouts  2.97 us (2%)
  other arithmetic  1.74 us (1%)
    psum x1, waiting for transfers between devices, shards(): summed = lax.psum(panels, 'tensor')  79.5 us
    all_to_all x1, waiting for transfers between devices, exchange_gather(): tiles = lax.all_to_all(tiles, axis, split_axis=0, concat_axis=0)  17.8 us
    all_to_all x1, starting transfers between devices, exchange_gather(): tiles = lax.all_to_all(tiles, axis, split_axis=0, concat_axis=0)  14.1 us
    dot_general x1, matrix products, shards(): jnp.einsum('stf,af->sta', hidden, proj_in, preferred_element_type=jnp.flo...  5.43 us
  transfers between devices with their start and end apart: 2, of which 2 were waited for; matrix products, arithmetic and copies ran while one was open for 0% of the time, Pallas kernels for 0%

profile of v2, /device:TPU:1, one launch (start us, length us, event | category | flops | bytes accessed | tf_op | source)
XLA Modules:
  0.0 139.8 jit_solution(12635366835619158650)
XLA Ops:
  6.5 0.0 copy-start
  6.5 0.0 all-reduce.2.cloned.1.call-start
  6.5 1.6 %copy-done = bf16[1,1024,1024]{2,1,0:T(8,128)(2,1)S(1)} copy-done((bf16[1,1024,1024]{2,1,0:T(8,128)(2,1)S(1)}, bf16[1,1024,1024]{2,1,0:T(8,128)(2,1)}, u32[]{:S(2)}) %copy-start) | copy-done | bytes 2097176
  8.1 1.7 %fusion.4 = f32[1,1024,64]{1,2,0:T(8,128)S(1)} fusion(bf16[64,1024]{1,0:T(8,128)(2,1)} %param.7, bf16[1,1024,1024]{2,1,0:T(8,128)(2,1)S(1)} %copy-done), kind=kOutput, calls=%fused_computation.4 | convolution fusion | flops 134217728 | bytes 2490368 | tf_op jit(solution)/shard_map/ste,be->stb/dot_general | solution.py:33
  9.8 5.4 %fusion.8 = f32[1,1024,64]{1,2,0:T(8,128)S(1)} fusion(bf16[64,3584]{1,0:T(8,128)(2,1)} %param.6, bf16[1,1024,3584]{2,1,0:T(8,128)(2,1)} %param.4), kind=kOutput, calls=%fused_computation.7 | convolution fusion | flops 469762048 | bytes 8060928 | tf_op jit(solution)/shard_map/stf,af->sta/dot_general | solution.py:32
  15.2 0.9 pad_maximum_fusion
  16.1 0.0 all-reduce.2.cloned.1.call-update
  16.1 79.5 %all-reduce.2.cloned.1.call-done = f32[1,1024,128]{1,2,0:T(8,128)} async-done(((f32[1,1024,128]{1,2,0:T(8,128)}), f32[1,1024,128]{1,2,0:T(8,128)}) %all-reduce.2.cloned.1.call-update) | async-done | bytes 524304 | tf_op jit(solution)/shard_map/psum | solution.py:35
  95.6 1.4 convolution_multiply_fusion.1
  97.0 0.1 stack_reshape.2
  97.1 1.3 stack.3
  98.4 14.1 %all-to-all-start = ((f32[32,1,4096]{2,1,0:T(1,128)}), f32[32,1,4096]{2,1,0:T(1,128)S(1)}, u32[]{:S(2)}, u32[]{:S(2)}) async-start(f32[32,1,4096]{2,1,0:T(1,128)} %stack.3), calls=%async_computation | async-start | bytes 1048576 | tf_op jit(solution)/shard_map/all_to_all | solution.py:11
  112.5 17.8 %all-to-all-done = f32[32,1,4096]{2,1,0:T(1,128)S(1)} async-done(((f32[32,1,4096]{2,1,0:T(1,128)}), f32[32,1,4096]{2,1,0:T(1,128)S(1)}, u32[]{:S(2)}, u32[]{:S(2)}) %all-to-all-start) | async-done | bytes 524320 | tf_op jit(solution)/shard_map/all_to_all | solution.py:11
  130.2 0.9 fusion.11
  131.8 1.1 fusion.7
  (4 shorter events, 0.1 us)
Async XLA Ops:
  6.5 1.6 %copy-start = (bf16[1,1024,1024]{2,1,0:T(8,128)(2,1)S(1)}, bf16[1,1024,1024]{2,1,0:T(8,128)(2,1)}, u32[]{:S(2)}) copy-start(bf16[1,1024,1024]{2,1,0:T(8,128)(2,1)} %param.5) | copy-start | bytes 6291460
  6.5 89.1 %all-reduce.2.cloned.1.call-start = ((), (), s32[]{:S(2)}) async-start(), calls=%async_computation.1 | async-start | bytes 1048576 | tf_op jit(solution)/shard_map/psum | solution.py:35
  98.4 31.9 %all-to-all-start = ((f32[32,1,4096]{2,1,0:T(1,128)}), f32[32,1,4096]{2,1,0:T(1,128)S(1)}, u32[]{:S(2)}, u32[]{:S(2)}) async-start(f32[32,1,4096]{2,1,0:T(1,128)} %stack.3), calls=%async_computation | async-start | bytes 1048576 | tf_op jit(solution)/shard_map/all_to_all | solution.py:11
Sparse Core Ops, SparseCore 0:
  16.2 79.3 all-reduce.1
